TPU v7x, 32 devices: a whole 2x2x4 slice. The times are simulated.
32 devices in a mesh: depth: 16 (over z, x, core), lat: 2 (over y).
Axes of the slice: x: 2, y: 2, z: 4, core: 2. Of those that a mesh axis runs over, the one named last changes fastest.
Arguments:
- waves_in: float32 [16, 4, 4, 16, 1024], P('depth', None, None, 'lat'), may hold values from -6 to 6
- surface_waves: float32 [4, 4, 16, 1024], P(None, None, 'lat'), may hold values from -6 to 6
- slowness: float32 [16, 4, 16, 1024], P('depth', None, 'lat'), may hold values from 0.22 to 0.67
- section_planes: int32 [16], P('depth'), may hold values from 1 to 4, 48 in all
- block_freqs: int32 [16, 4], P('depth'), may hold values from 0 to 63
- surface_freqs: int32 [4], replicated, may hold values from 0 to 63
Outputs:
- waves_out: float32 [16, 4, 4, 16, 1024], P('depth', None, None, 'lat')
- image: float32 [16, 4, 16, 1024], P('depth', None, 'lat')
Inputs may be any that keep to these rules, and one draw needn't show every extreme that they name: `section_planes`: some section has exactly 4 active planes; the counts sum to 48.
All inputs are finite; a program needn't handle non-finite values. No bound on the sum of `section_planes` on one device may be relied on, other than what follows from the above.
Results may differ from a plain program's by a relative error of at most 0.0003.
Values sent between devices are 32-bit elements; how exact they have to be, the bound alone decides.
A program may use at most 64 MiB of HBM per device.

v0:
```python
import math

import jax
import jax.numpy as jnp
from jax import lax
from jax.sharding import PartitionSpec as P

DEPTH_STEP = 0.02
SMOOTHING = 0.4
BASE_HERTZ = 8.0
HERTZ_STEP = 0.5
DIFFRACTION_TOP = 0.2


def extended(x, sides, width):
    for axis, dim in sides:
        devices, length = (lax.axis_size(axis), x.shape[dim])
        up = [(i, (i + 1) % devices) for i in range(devices - 1)]
        down = [(j, i) for i, j in up]
        last = lax.slice_in_dim(x, length - width, length, axis=dim)
        first = lax.slice_in_dim(x, 0, width, axis=dim)
        before = lax.ppermute(last, axis, up)
        after = lax.ppermute(first, axis, down)
        x = jnp.concatenate([before, x, after], axis=dim)
    return x


def from_behind(value, axis, steps):
    count = lax.axis_size(axis)
    first, last = (max(0, -steps), min(count, count - steps))
    return lax.ppermute(value, axis, [(source, source + steps) for source in range(first, last)])


def angular_of(freqs):
    return 2.0 * math.pi * (BASE_HERTZ + HERTZ_STEP * freqs.astype(jnp.float32))


def diffraction_of(pulsation):
    return DIFFRACTION_TOP * (2.0 * math.pi * BASE_HERTZ) / pulsation


def phase_shifted(fields, slowness_slab, pulsation):
    phase = pulsation[:, None, None] * slowness_slab[None] * DEPTH_STEP
    cosine_part = jnp.cos(phase)
    sine_part = jnp.sin(phase)
    source_real = fields[:, 0] * cosine_part - fields[:, 1] * sine_part
    source_imag = fields[:, 0] * sine_part + fields[:, 1] * cosine_part
    receiver_real = fields[:, 2] * cosine_part + fields[:, 3] * sine_part
    receiver_imag = fields[:, 3] * cosine_part - fields[:, 2] * sine_part
    return jnp.stack([source_real, source_imag, receiver_real, receiver_imag], 1)


def filtered(fields, second_diff, diffraction):
    source_real = fields[:, 0] + SMOOTHING * second_diff[:, 0] - diffraction * second_diff[:, 1]
    source_imag = fields[:, 1] + SMOOTHING * second_diff[:, 1] + diffraction * second_diff[:, 0]
    receiver_real = fields[:, 2] + SMOOTHING * second_diff[:, 2] + diffraction * second_diff[:, 3]
    receiver_imag = fields[:, 3] + SMOOTHING * second_diff[:, 3] - diffraction * second_diff[:, 2]
    return jnp.stack([source_real, source_imag, receiver_real, receiver_imag], 1)


def across_columns(fields, diffraction):
    padded = jnp.pad(fields, ((0, 0), (0, 0), (0, 0), (1, 1)))
    return filtered(fields, padded[..., 2:] + padded[..., :-2] - 2.0 * fields, diffraction)


def correlation(fields):
    return jnp.sum(fields[:, 0] * fields[:, 2] + fields[:, 1] * fields[:, 3], axis=0)


def prepare_slab(slowness_slab):
    return extended(slowness_slab, (("lat", 1),), slowness_slab.shape[0])


def run_section(fields, prepared_slab, active_planes, pulsation):
    plane_count = active_planes.shape[0]
    strip_rows = fields.shape[2]
    block_size = fields.shape[0]
    diffraction = diffraction_of(pulsation)[:, None, None]
    images = []
    widened = extended(fields, (("lat", 2),), plane_count)
    first_row = lax.axis_index("lat") * strip_rows - plane_count
    position = first_row + jnp.arange(strip_rows + 2 * plane_count)
    inside = ((position >= 0) & (position < strip_rows * lax.axis_size("lat"))).astype(jnp.float32)[
        :, None
    ]
    for depth_slot in range(plane_count):
        updated = phase_shifted(widened, prepared_slab[depth_slot], pulsation)
        padded = jnp.pad(updated, ((0, 0), (0, 0), (1, 1), (0, 0)))
        updated = (
            filtered(updated, padded[:, :, 2:] + padded[:, :, :-2] - 2.0 * updated, diffraction)
            * inside
        )
        updated = across_columns(updated, diffraction)
        active_now = active_planes[depth_slot]
        widened = jnp.where(active_now > 0, updated, widened)
        middle = updated[:, :, plane_count : plane_count + strip_rows]
        images.append(active_now * correlation(middle) / block_size)
    return (widened[:, :, plane_count : plane_count + strip_rows], jnp.stack(images))


def local(waves_in, surface_waves, slowness, section_planes, block_freqs, surface_freqs):
    plane_count = slowness.shape[1]
    active_planes = (jnp.arange(plane_count) < section_planes[0]).astype(jnp.float32)
    own_pulsation = angular_of(block_freqs[0])
    surface_pulsation = angular_of(surface_freqs)
    own_fields = waves_in[0]
    own_slab = slowness[0]
    prepared_slab = prepare_slab(own_slab)
    at_surface = lax.axis_index("depth") == 0
    first_out, first_image = run_section(own_fields, prepared_slab, active_planes, own_pulsation)
    previous, previous_pulsation = from_behind((first_out, own_pulsation), "depth", 1)
    second_in = jnp.where(at_surface, surface_waves, previous)
    second_pulsation = jnp.where(at_surface, surface_pulsation, previous_pulsation)
    waves_out, second_image = run_section(second_in, prepared_slab, active_planes, second_pulsation)
    return (waves_out[None], (first_image + second_image)[None])


def solution(mesh):
    return jax.shard_map(
        local,
        mesh=mesh,
        in_specs=(
            P("depth", None, None, "lat", None),
            P(None, None, "lat", None),
            P("depth", None, "lat", None),
            P("depth"),
            P("depth", None),
            P(),
        ),
        out_specs=(P("depth", None, None, "lat", None), P("depth", None, "lat", None)),
        check_vma=False,
    )
```

profile of v0, /device:TPU:8, one launch (start us, length us, event | category | flops | bytes accessed | tf_op | source)
XLA Modules:
  0.0 78.8 jit_solution(1043663925938828783)
XLA Ops:
  0.7 0.7 multiply_bitcast_fusion.8
  1.4 1.9 %collective-permute-start.7 = (f32[4]{0:T(128)S(1)}, f32[4]{0:T(128)S(1)}, u32[]{:S(2)}, u32[]{:S(2)}) collective-permute-start(f32[4]{0:T(128)S(1)} %multiply_bitcast_fusion.8), channel_id=1, source_target_pairs={{0,2},{2,4},{4,6},{6,8},{8,10},{10,12},{12,14},{14,16},{16,18},{18... | collective-permute-start | bytes 56 | tf_op jit(solution)/shard_map/ppermute | solution.py:31
  3.3 1.0 %fusion.99 = (f32[4,4,1024]{2,1,0:T(4,128)S(1)}, f32[4,4,1024]{2,1,0:T(4,128)S(1)}) fusion(f32[4,8,1024]{2,1,0:T(8,128)} %bitcast.41), kind=kLoop, calls=%fused_computation.304 | loop fusion | bytes 262144 | tf_op jit(solution)/shard_map/slice | solution.py:20
  4.3 3.4 %collective-permute-start.2 = (f32[4,4,1024]{2,1,0:T(4,128)S(1)}, f32[4,4,1024]{2,1,0:T(4,128)S(1)}, u32[]{:S(2)}, u32[]{:S(2)}) collective-permute-start(f32[4,4,1024]{2,1,0:T(4,128)S(1)} %get-tuple-element.108), channel_id=1, source_target_pairs={{0,1},{2,3},{4,5},{6,7},{8,9},{10,11},{12,13},{14,15},{16,17},{18,... | collective-permute-start | bytes 196616 | tf_op jit(solution)/shard_map/ppermute | solution.py:22
  7.7 1.3 %collective-permute-start.3 = (f32[4,4,1024]{2,1,0:T(4,128)S(1)}, f32[4,4,1024]{2,1,0:T(4,128)S(1)}, u32[]{:S(2)}, u32[]{:S(2)}) collective-permute-start(f32[4,4,1024]{2,1,0:T(4,128)S(1)} %get-tuple-element.109), channel_id=1, source_target_pairs={{1,0},{3,2},{5,4},{7,6},{9,8},{11,10},{13,12},{15,14},{17,16},{19,... | collective-permute-start | bytes 196616 | tf_op jit(solution)/shard_map/ppermute | solution.py:23
  9.0 1.4 %fusion.98 = (f32[4,4,4,1024]{3,2,1,0:T(4,128)S(1)}, f32[4,4,4,1024]{3,2,1,0:T(4,128)S(1)}) fusion(f32[4,4,8,1024]{3,2,1,0:T(8,128)} %bitcast.38), kind=kLoop, calls=%fused_computation.303 | loop fusion | bytes 1048576 | tf_op jit(solution)/shard_map/slice | solution.py:20
  10.4 4.6 %collective-permute-start = (f32[4,4,4,1024]{3,2,1,0:T(4,128)S(1)}, f32[4,4,4,1024]{3,2,1,0:T(4,128)S(1)}, u32[]{:S(2)}, u32[]{:S(2)}) collective-permute-start(f32[4,4,4,1024]{3,2,1,0:T(4,128)S(1)} %get-tuple-element.102), channel_id=1, source_target_pairs={{0,1},{2,3},{4,5},{6,7},{8,9},{10,11},{12,13},{14,15},{16,17},{18,... | collective-permute-start | bytes 786440 | tf_op jit(solution)/shard_map/ppermute | solution.py:22
  15.0 1.3 %collective-permute-start.1 = (f32[4,4,4,1024]{3,2,1,0:T(4,128)S(1)}, f32[4,4,4,1024]{3,2,1,0:T(4,128)S(1)}, u32[]{:S(2)}, u32[]{:S(2)}) collective-permute-start(f32[4,4,4,1024]{3,2,1,0:T(4,128)S(1)} %get-tuple-element.103), channel_id=1, source_target_pairs={{1,0},{3,2},{5,4},{7,6},{9,8},{11,10},{13,12},{15,14},{17,16},{19,... | collective-permute-start | bytes 786440 | tf_op jit(solution)/shard_map/ppermute | solution.py:23
  17.0 0.7 fusion.100
  20.3 1.2 %collective-permute-done = f32[4,4,4,1024]{3,2,1,0:T(4,128)S(1)} collective-permute-done((f32[4,4,4,1024]{3,2,1,0:T(4,128)S(1)}, f32[4,4,4,1024]{3,2,1,0:T(4,128)S(1)}, u32[]{:S(2)}, u32[]{:S(2)}) %collective-permute-start) | collective-permute-done | bytes 262176 | tf_op jit(solution)/shard_map/ppermute | solution.py:22
  21.6 4.3 %collective-permute-done.1 = f32[4,4,4,1024]{3,2,1,0:T(4,128)S(1)} collective-permute-done((f32[4,4,4,1024]{3,2,1,0:T(4,128)S(1)}, f32[4,4,4,1024]{3,2,1,0:T(4,128)S(1)}, u32[]{:S(2)}, u32[]{:S(2)}) %collective-permute-start.1) | collective-permute-done | bytes 262176 | tf_op jit(solution)/shard_map/ppermute | solution.py:23
  26.0 1.2 %multiply_subtract_fusion.31 = (f32[4,1,16,1024]{3,2,1,0:T(8,128)S(1)}, f32[4,1,16,1024]{3,2,1,0:T(8,128)S(1)}, f32[4,1,16,1024]{3,2,1,0:T(8,128)S(1)}, f32[4,1,16,1024]{3,2,1,0:T(8,128)S(1)}) fusion(f32[4,4,16,1024]{3,2,1,0:T(8,128)S(1)} %pad_maximum_fusion, f32[16,1024]{1,0:T(8,128)S(1)} %get-tuple-element.107, f32[4]{0:T(128)S(1)} %multiply_bitcast_fusion.8), kind=kLoop, calls=%fused_computation.246 | loop fusion | flops 917504 | bytes 2162704 | tf_op jit(solution)/shard_map/sub | solution.py:46
  27.4 0.2 fusion.17
  27.6 0.3 multiply_subtract_fusion.29
  28.1 0.6 fusion.1
  28.8 0.3 fusion.64
  29.1 0.3 maximum_select_fusion
  29.4 1.2 %multiply_subtract_fusion.27 = (f32[4,1,16,1024]{3,2,1,0:T(8,128)S(1)}, f32[4,1,16,1024]{3,2,1,0:T(8,128)S(1)}, f32[4,1,16,1024]{3,2,1,0:T(8,128)S(1)}, f32[4,1,16,1024]{3,2,1,0:T(8,128)S(1)}) fusion(f32[4,4,16,1024]{3,2,1,0:T(8,128)S(1)} %maximum_select_fusion, f32[16,1024]{1,0:T(8,128)S(1)} %get-tuple-element.106, f32[4]{0:T(128)S(1)} %multiply_bitcast_fusion.8), kind=kLoop, calls=%fused_computation.235 | loop fusion | flops 917504 | bytes 2162704 | tf_op jit(solution)/shard_map/sub | solution.py:46
  30.7 0.2 fusion.19
  31.0 0.3 multiply_subtract_fusion.25
  31.5 0.6 fusion.3
  32.1 0.4 fusion.60
  32.6 1.2 %multiply_subtract_fusion.23 = (f32[4,1,16,1024]{3,2,1,0:T(8,128)S(1)}, f32[4,1,16,1024]{3,2,1,0:T(8,128)S(1)}, f32[4,1,16,1024]{3,2,1,0:T(8,128)S(1)}, f32[4,1,16,1024]{3,2,1,0:T(8,128)S(1)}) fusion(f32[4,4,16,1024]{3,2,1,0:T(8,128)S(1)} %maximum_select_fusion.1, f32[16,1024]{1,0:T(8,128)S(1)} %get-tuple-element.105, f32[4]{0:T(128)S(1)} %multiply_bitcast_fusion.8), kind=kLoop, calls=%fused_computation.224 | loop fusion | flops 917504 | bytes 2162704 | tf_op jit(solution)/shard_map/sub | solution.py:46
  34.0 0.2 fusion.21
  34.2 0.3 multiply_subtract_fusion.21
  34.8 0.6 fusion.5
  35.4 0.4 fusion.56
  35.7 0.4 maximum_select_fusion.2
  36.1 1.2 %multiply_subtract_fusion.19 = (f32[4,1,16,1024]{3,2,1,0:T(8,128)S(1)}, f32[4,1,16,1024]{3,2,1,0:T(8,128)S(1)}, f32[4,1,16,1024]{3,2,1,0:T(8,128)S(1)}, f32[4,1,16,1024]{3,2,1,0:T(8,128)S(1)}) fusion(f32[4,4,16,1024]{3,2,1,0:T(8,128)S(1)} %maximum_select_fusion.2, f32[16,1024]{1,0:T(8,128)S(1)} %get-tuple-element.104, f32[4]{0:T(128)S(1)} %multiply_bitcast_fusion.8), kind=kLoop, calls=%fused_computation.213 | loop fusion | flops 917504 | bytes 2162704 | tf_op jit(solution)/shard_map/sub | solution.py:46
  37.5 0.2 fusion.23
  37.7 0.3 multiply_subtract_fusion.17
  38.3 0.6 fusion.7
  38.9 0.3 fusion.52
  39.4 2.1 %collective-permute-start.4 = (f32[4,4,8,1024]{3,2,1,0:T(8,128)S(1)}, f32[4,4,8,1024]{3,2,1,0:T(8,128)S(1)}, u32[]{:S(2)}, u32[]{:S(2)}) collective-permute-start(f32[4,4,8,1024]{3,2,1,0:T(8,128)S(1)} %slice_select_fusion.1), channel_id=1, source_target_pairs={{0,2},{2,4},{4,6},{6,8},{8,10},{10,12},{12,14},{14,16},{16,18},{18... | collective-permute-start | bytes 1572872 | tf_op jit(solution)/shard_map/ppermute | solution.py:31
  41.7 0.6 multiply_bitcast_fusion.6
  42.4 8.6 %collective-permute-done.4 = f32[4,4,8,1024]{3,2,1,0:T(8,128)S(1)} collective-permute-done((f32[4,4,8,1024]{3,2,1,0:T(8,128)S(1)}, f32[4,4,8,1024]{3,2,1,0:T(8,128)S(1)}, u32[]{:S(2)}, u32[]{:S(2)}) %collective-permute-start.4) | collective-permute-done | bytes 524320 | tf_op jit(solution)/shard_map/ppermute | solution.py:31
  51.2 1.5 %collective-permute-start.5 = (f32[4,4,4,1024]{3,2,1,0:T(4,128)S(1)}, f32[4,4,4,1024]{3,2,1,0:T(4,128)S(1)}, u32[]{:S(2)}, u32[]{:S(2)}) collective-permute-start(f32[4,4,4,1024]{3,2,1,0:T(4,128)S(1)} %get-tuple-element.100), channel_id=1, source_target_pairs={{0,1},{2,3},{4,5},{6,7},{8,9},{10,11},{12,13},{14,15},{16,17},{18,... | collective-permute-start | bytes 786440 | tf_op jit(solution)/shard_map/ppermute | solution.py:22
  52.7 1.5 %collective-permute-start.6 = (f32[4,4,4,1024]{3,2,1,0:T(4,128)S(1)}, f32[4,4,4,1024]{3,2,1,0:T(4,128)S(1)}, u32[]{:S(2)}, u32[]{:S(2)}) collective-permute-start(f32[4,4,4,1024]{3,2,1,0:T(4,128)S(1)} %get-tuple-element.101), channel_id=1, source_target_pairs={{1,0},{3,2},{5,4},{7,6},{9,8},{11,10},{13,12},{15,14},{17,16},{19,... | collective-permute-start | bytes 786440 | tf_op jit(solution)/shard_map/ppermute | solution.py:23
  54.2 1.3 %multiply_bitcast_fusion.4 = (f32[1,1,8,1024]{3,2,1,0:T(8,128)S(1)}, f32[1,1,8,1024]{3,2,1,0:T(8,128)S(1)}) fusion(f32[8,1024]{1,0:T(8,128)S(1)} %fusion.90, f32[]{:T(128)} %bitcast.1, f32[8,1024]{1,0:T(8,128)S(1)} %fusion.92, f32[]{:T(128)} %bitcast.2), kind=kLoop, calls=%fused_computation.292 | loop fusion | flops 32768 | bytes 131080 | tf_op jit(solution)/shard_map/stack | solution.py:98
  55.5 1.2 %collective-permute-done.5 = f32[4,4,4,1024]{3,2,1,0:T(4,128)S(1)} collective-permute-done((f32[4,4,4,1024]{3,2,1,0:T(4,128)S(1)}, f32[4,4,4,1024]{3,2,1,0:T(4,128)S(1)}, u32[]{:S(2)}, u32[]{:S(2)}) %collective-permute-start.5) | collective-permute-done | bytes 262176 | tf_op jit(solution)/shard_map/ppermute | solution.py:22
  56.8 4.2 %collective-permute-done.6 = f32[4,4,4,1024]{3,2,1,0:T(4,128)S(1)} collective-permute-done((f32[4,4,4,1024]{3,2,1,0:T(4,128)S(1)}, f32[4,4,4,1024]{3,2,1,0:T(4,128)S(1)}, u32[]{:S(2)}, u32[]{:S(2)}) %collective-permute-start.6) | collective-permute-done | bytes 262176 | tf_op jit(solution)/shard_map/ppermute | solution.py:23
  61.1 1.2 %multiply_subtract_fusion.15 = (f32[4,1,16,1024]{3,2,1,0:T(8,128)S(1)}, f32[4,1,16,1024]{3,2,1,0:T(8,128)S(1)}, f32[4,1,16,1024]{3,2,1,0:T(8,128)S(1)}, f32[4,1,16,1024]{3,2,1,0:T(8,128)S(1)}) fusion(f32[4,4,16,1024]{3,2,1,0:T(8,128)S(1)} %pad_maximum_fusion.5, f32[4]{0:T(128)S(1)} %get-tuple-element.3, f32[16,1024]{1,0:T(8,128)S(1)} %get-tuple-element.107), kind=kLoop, calls=%fused_computation.202 | loop fusion | flops 917504 | bytes 2162704 | tf_op jit(solution)/shard_map/sub | solution.py:46
  62.7 0.3 multiply_subtract_fusion.13
  63.2 0.6 fusion.9
  63.8 0.4 fusion.48
  64.3 0.3 maximum_select_fusion.3
  64.5 1.2 %multiply_subtract_fusion.11 = (f32[4,1,16,1024]{3,2,1,0:T(8,128)S(1)}, f32[4,1,16,1024]{3,2,1,0:T(8,128)S(1)}, f32[4,1,16,1024]{3,2,1,0:T(8,128)S(1)}, f32[4,1,16,1024]{3,2,1,0:T(8,128)S(1)}) fusion(f32[4,4,16,1024]{3,2,1,0:T(8,128)S(1)} %maximum_select_fusion.3, f32[4]{0:T(128)S(1)} %get-tuple-element.3, f32[16,1024]{1,0:T(8,128)S(1)} %get-tuple-element.106), kind=kLoop, calls=%fused_computation.191 | loop fusion | flops 917504 | bytes 2162704 | tf_op jit(solution)/shard_map/sub | solution.py:46
  66.1 0.3 multiply_subtract_fusion.9
  66.7 0.6 fusion.11
  67.3 0.4 fusion.44
  67.9 1.2 %multiply_subtract_fusion.7 = (f32[4,1,16,1024]{3,2,1,0:T(8,128)S(1)}, f32[4,1,16,1024]{3,2,1,0:T(8,128)S(1)}, f32[4,1,16,1024]{3,2,1,0:T(8,128)S(1)}, f32[4,1,16,1024]{3,2,1,0:T(8,128)S(1)}) fusion(f32[4,4,16,1024]{3,2,1,0:T(8,128)S(1)} %maximum_select_fusion.4, f32[4]{0:T(128)S(1)} %get-tuple-element.3, f32[16,1024]{1,0:T(8,128)S(1)} %get-tuple-element.105), kind=kLoop, calls=%fused_computation.180 | loop fusion | flops 917504 | bytes 2162704 | tf_op jit(solution)/shard_map/sub | solution.py:46
  69.5 0.3 multiply_subtract_fusion.5
  70.0 0.6 fusion.13
  70.6 0.3 fusion.40
  70.9 0.4 maximum_select_fusion.5
  71.4 1.2 %multiply_subtract_fusion.3 = (f32[4,1,16,1024]{3,2,1,0:T(8,128)S(1)}, f32[4,1,16,1024]{3,2,1,0:T(8,128)S(1)}, f32[4,1,16,1024]{3,2,1,0:T(8,128)S(1)}, f32[4,1,16,1024]{3,2,1,0:T(8,128)S(1)}) fusion(f32[4,4,16,1024]{3,2,1,0:T(8,128)S(1)} %maximum_select_fusion.5, f32[4]{0:T(128)S(1)} %get-tuple-element.3, f32[16,1024]{1,0:T(8,128)S(1)} %get-tuple-element.104), kind=kLoop, calls=%fused_computation.169 | loop fusion | flops 917504 | bytes 2162704 | tf_op jit(solution)/shard_map/sub | solution.py:46
  73.0 0.3 multiply_subtract_fusion.1
  73.5 0.6 fusion.15
  74.1 0.3 fusion.36
  74.5 1.0 %fusion.32 = f32[1,4,4,8,1024]{4,3,2,1,0:T(8,128)} fusion(f32[4,4,16,1024]{3,2,1,0:T(8,128)S(1)} %maximum_select_fusion.5, f32[4,1,16,1024]{3,2,1,0:T(8,128)S(1)} %get-tuple-element.7, f32[4,1,16,1024]{3,2,1,0:T(8,128)S(1)} %get-tuple-element.5, f32[4,1,16,1024]{3,2,1,0:T(8,128)S(1)} %get-tuple-element.6, f32[4,1,16,1024]{3,2,1,0:T(8,128)S(1)} %get-tuple-element.4, ...), kind=kLoop, calls=%fused_computation.89 | loop fusion | flops 524288 | bytes 2097153 | tf_op jit(solution)/shard_map/broadcast_in_dim | solution.py:115
  75.6 0.6 multiply_bitcast_fusion.2
  76.2 0.6 multiply_bitcast_fusion.3
  76.9 1.3 %multiply_bitcast_fusion = (f32[1,1,8,1024]{3,2,1,0:T(8,128)S(1)}, f32[1,1,8,1024]{3,2,1,0:T(8,128)S(1)}) fusion(f32[8,1024]{1,0:T(8,128)S(1)} %fusion.82, f32[]{:T(128)} %bitcast.1, f32[8,1024]{1,0:T(8,128)S(1)} %fusion.84, f32[]{:T(128)} %bitcast.2), kind=kLoop, calls=%fused_computation.288 | loop fusion | flops 32768 | bytes 131080 | tf_op jit(solution)/shard_map/stack | solution.py:98
  78.1 0.7 maximum_add_fusion
  (54 shorter events, 5.1 us)
Async XLA Ops:
  0.6 15.6 %copy-start.4 = (s32[1,4]{1,0:T(1,128)S(1)}, s32[1,4]{1,0:T(1,128)}, u32[]{:S(2)}) copy-start(s32[1,4]{1,0:T(1,128)} %param.10) | copy-start | bytes 52
  0.6 19.6 %copy-start.2 = (f32[1,4,8,1024]{3,2,1,0:T(8,128)S(1)}, f32[1,4,8,1024]{3,2,1,0:T(8,128)}, u32[]{:S(2)}) copy-start(f32[1,4,8,1024]{3,2,1,0:T(8,128)} %param.8) | copy-start | bytes 393220
  0.7 19.5 %copy-start.3 = (s32[4]{0:T(128)S(1)}, s32[4]{0:T(128)}, u32[]{:S(2)}) copy-start(s32[4]{0:T(128)} %param.11) | copy-start | bytes 52
  1.4 18.8 %collective-permute-start.7 = (f32[4]{0:T(128)S(1)}, f32[4]{0:T(128)S(1)}, u32[]{:S(2)}, u32[]{:S(2)}) collective-permute-start(f32[4]{0:T(128)S(1)} %multiply_bitcast_fusion.8), channel_id=1, source_target_pairs={{0,2},{2,4},{4,6},{6,8},{8,10},{10,12},{12,14},{14,16},{16,18},{18... | collective-permute-start | bytes 56 | tf_op jit(solution)/shard_map/ppermute | solution.py:31
  4.3 15.9 %collective-permute-start.2 = (f32[4,4,1024]{2,1,0:T(4,128)S(1)}, f32[4,4,1024]{2,1,0:T(4,128)S(1)}, u32[]{:S(2)}, u32[]{:S(2)}) collective-permute-start(f32[4,4,1024]{2,1,0:T(4,128)S(1)} %get-tuple-element.108), channel_id=1, source_target_pairs={{0,1},{2,3},{4,5},{6,7},{8,9},{10,11},{12,13},{14,15},{16,17},{18,... | collective-permute-start | bytes 196616 | tf_op jit(solution)/shard_map/ppermute | solution.py:22
  7.7 12.5 %collective-permute-start.3 = (f32[4,4,1024]{2,1,0:T(4,128)S(1)}, f32[4,4,1024]{2,1,0:T(4,128)S(1)}, u32[]{:S(2)}, u32[]{:S(2)}) collective-permute-start(f32[4,4,1024]{2,1,0:T(4,128)S(1)} %get-tuple-element.109), channel_id=1, source_target_pairs={{1,0},{3,2},{5,4},{7,6},{9,8},{11,10},{13,12},{15,14},{17,16},{19,... | collective-permute-start | bytes 196616 | tf_op jit(solution)/shard_map/ppermute | solution.py:23
  9.0 16.8 %copy-start = (f32[1,4,4,8,1024]{4,3,2,1,0:T(8,128)S(1)}, f32[1,4,4,8,1024]{4,3,2,1,0:T(8,128)}, u32[]{:S(2)}) copy-start(f32[1,4,4,8,1024]{4,3,2,1,0:T(8,128)} %param.6) | copy-start | bytes 1572868
  10.4 11.2 %collective-permute-start = (f32[4,4,4,1024]{3,2,1,0:T(4,128)S(1)}, f32[4,4,4,1024]{3,2,1,0:T(4,128)S(1)}, u32[]{:S(2)}, u32[]{:S(2)}) collective-permute-start(f32[4,4,4,1024]{3,2,1,0:T(4,128)S(1)} %get-tuple-element.102), channel_id=1, source_target_pairs={{0,1},{2,3},{4,5},{6,7},{8,9},{10,11},{12,13},{14,15},{16,17},{18,... | collective-permute-start | bytes 786440 | tf_op jit(solution)/shard_map/ppermute | solution.py:22
  15.0 10.9 %collective-permute-start.1 = (f32[4,4,4,1024]{3,2,1,0:T(4,128)S(1)}, f32[4,4,4,1024]{3,2,1,0:T(4,128)S(1)}, u32[]{:S(2)}, u32[]{:S(2)}) collective-permute-start(f32[4,4,4,1024]{3,2,1,0:T(4,128)S(1)} %get-tuple-element.103), channel_id=1, source_target_pairs={{1,0},{3,2},{5,4},{7,6},{9,8},{11,10},{13,12},{15,14},{17,16},{19,... | collective-permute-start | bytes 786440 | tf_op jit(solution)/shard_map/ppermute | solution.py:23
  39.4 11.5 %copy-start.1 = (f32[4,4,8,1024]{3,2,1,0:T(8,128)S(1)}, f32[4,4,8,1024]{3,2,1,0:T(8,128)}, u32[]{:S(2)}) copy-start(f32[4,4,8,1024]{3,2,1,0:T(8,128)} %param.7) | copy-start | bytes 1572868
  39.4 11.5 %collective-permute-start.4 = (f32[4,4,8,1024]{3,2,1,0:T(8,128)S(1)}, f32[4,4,8,1024]{3,2,1,0:T(8,128)S(1)}, u32[]{:S(2)}, u32[]{:S(2)}) collective-permute-start(f32[4,4,8,1024]{3,2,1,0:T(8,128)S(1)} %slice_select_fusion.1), channel_id=1, source_target_pairs={{0,2},{2,4},{4,6},{6,8},{8,10},{10,12},{12,14},{14,16},{16,18},{18... | collective-permute-start | bytes 1572872 | tf_op jit(solution)/shard_map/ppermute | solution.py:31
  51.2 5.6 %collective-permute-start.5 = (f32[4,4,4,1024]{3,2,1,0:T(4,128)S(1)}, f32[4,4,4,1024]{3,2,1,0:T(4,128)S(1)}, u32[]{:S(2)}, u32[]{:S(2)}) collective-permute-start(f32[4,4,4,1024]{3,2,1,0:T(4,128)S(1)} %get-tuple-element.100), channel_id=1, source_target_pairs={{0,1},{2,3},{4,5},{6,7},{8,9},{10,11},{12,13},{14,15},{16,17},{18,... | collective-permute-start | bytes 786440 | tf_op jit(solution)/shard_map/ppermute | solution.py:22
  52.7 8.3 %collective-permute-start.6 = (f32[4,4,4,1024]{3,2,1,0:T(4,128)S(1)}, f32[4,4,4,1024]{3,2,1,0:T(4,128)S(1)}, u32[]{:S(2)}, u32[]{:S(2)}) collective-permute-start(f32[4,4,4,1024]{3,2,1,0:T(4,128)S(1)} %get-tuple-element.101), channel_id=1, source_target_pairs={{1,0},{3,2},{5,4},{7,6},{9,8},{11,10},{13,12},{15,14},{17,16},{19,... | collective-permute-start | bytes 786440 | tf_op jit(solution)/shard_map/ppermute | solution.py:23
where the time goes:
time: 79.3 us; the launch traced here: 78.8 us
  other arithmetic  34 us (43%)
  waiting for transfers between devices  19.5 us (25%)
  starting transfers between devices  17.5 us (22%)
  between operations  4.59 us (6%)
  local copies, waits for them, and re-layouts  3.19 us (4%)
    sub x8, other arithmetic, phase_shifted(): source_real = fields[:, 0] * cosine_part - fields[:, 1] * sine_part  9.83 us
    ppermute x3, starting transfers between devices, extended(): before = lax.ppermute(last, axis, up)  9.45 us
    ppermute x2, waiting for transfers between devices, from_behind(): lax.ppermute(value, axis, [(source, source + steps) for source in range(f...  8.61 us
    ppermute x3, waiting for transfers between devices, extended(): after = lax.ppermute(first, axis, down)  8.43 us
    sub x16, other arithmetic, filtered(): fields[:, 0] + SMOOTHING * second_diff[:, 0]  5.36 us
    sub x8, other arithmetic, across_columns(): padded[..., 2:] + padded[..., :-2] - 2.0 * fields  4.88 us
    another operation x5, other arithmetic, run_section(): jnp.stack(images)  4.44 us
    ppermute x3, starting transfers between devices, extended(): after = lax.ppermute(first, axis, down)  4.06 us
  transfers between devices with their start and end apart: 8, of which 5 were waited for; matrix products, arithmetic and copies ran while one was open for 7% of the time, Pallas kernels for 0%

commit v1 on v0

v1 whole, which is shorter than its diff:
```python
import functools
import math

import jax
import jax.numpy as jnp
from jax import lax
from jax.experimental import pallas as pl
from jax.experimental.pallas import tpu as pltpu
from jax.sharding import PartitionSpec as P

DEPTH_STEP = 0.02
SMOOTHING = 0.4
BASE_HERTZ = 8.0
HERTZ_STEP = 0.5
DIFFRACTION_TOP = 0.2
MIDDLE_SLOWNESS = 0.445
SIN = (0.9999999998446159, -0.16666666052254658, 0.008333294444188614, -0.0001983264692424553, 2.6775178137139403e-06)
COS = (0.9999999982977188, -0.4999999326780431, 0.04166624044803908, -0.0013879434435051892, 2.394331932466174e-05)
SUB, LANE = 8, 128
TILE = (SUB, LANE)


def horner(coefficients, t):
    value = coefficients[-1] * t + coefficients[-2]
    for c in coefficients[-3::-1]:
        value = value * t + c
    return value


def sin_cos(x):
    t = x * x
    return x * horner(SIN, t), horner(COS, t)


def constants_of(omega):
    beta = DIFFRACTION_TOP * (2.0 * math.pi * BASE_HERTZ) / omega
    rate = omega * DEPTH_STEP
    half_sin, half_cos = sin_cos(rate * (0.5 * MIDDLE_SLOWNESS))
    centre_sin, centre_cos = 2.0 * half_sin * half_cos, 1.0 - 2.0 * half_sin * half_sin
    norm = SMOOTHING * SMOOTHING + beta * beta
    g_re, g_im = SMOOTHING / norm - 2.0, -beta / norm
    a_re, a_im = SMOOTHING * SMOOTHING - beta * beta, 2.0 * SMOOTHING * beta
    k_re = a_re * centre_cos - a_im * centre_sin
    k_im = a_re * centre_sin + a_im * centre_cos
    return rate, g_re, g_im, k_re, k_im


def kernel(
    axes, waves, surface, slowness, planes_ref, freqs, surface_freqs, waves_out, image_out,
    nat, nat_surface, nat_slow, window, window2, slow, states, outgoing, omegas, omegas2, image, nat_out, nat_image,
    in_sem, out_sem, slow_send, slow_recv, halo_send, halo_recv, depth_send, depth_recv, omega_sem,
):
    sections, strips = axes
    s, l = lax.axis_index("depth"), lax.axis_index("lat")
    fb, plane_count = waves.shape[1], slowness.shape[1]
    halo = plane_count
    strip = waves.shape[3]
    folded = strips == 2
    top = 0 if folded else halo
    width = top + strip + halo
    following, previous = {"depth": lax.rem(s + 1, sections)}, {"depth": lax.rem(s + sections - 1, sections)}
    has_next, has_previous = s < sections - 1, s > 0

    if folded:
        other = {"lat": 1 - l}
        sides = [(None, None, other, [(strip - 1 - i, strip + i, 1) for i in range(halo)])]
    else:
        down, up = {"lat": lax.rem(l + 1, strips)}, {"lat": lax.rem(l + strips - 1, strips)}
        sides = [
            (l < strips - 1, l > 0, down, [(top + strip - halo, 0, halo)]),
            (l > 0, l < strips - 1, up, [(top, top + strip, halo)]),
        ]

    def run_if(condition, body):
        if condition is None:
            body()
        else:
            pl.when(condition)(body)

    def halo_copies(source, target, send, recv, partner, copies, first):
        return [
            pltpu.make_async_remote_copy(
                src_ref=source.at[pl.ds(row, rows)], dst_ref=target.at[pl.ds(place, rows)],
                send_sem=send.at[first + i], recv_sem=recv.at[first + i],
                device_id=partner, device_id_type=pl.DeviceIdType.MESH,
            )
            for i, (row, place, rows) in enumerate(copies)
        ]

    def halos(buffer, send, recv, action):
        first = 0
        for can_send, can_receive, partner, copies in sides:
            descriptors = halo_copies(buffer, buffer, send, recv, partner, copies, first)
            first += len(copies)

            def act(descriptors=descriptors):
                for copy in descriptors:
                    getattr(copy, action)()

            run_if(can_receive if action == "wait_recv" else can_send, act)

    def place_of(i):
        return i + l * (strip - 1 - 2 * i) if folded else i

    def natural(source, target, send, inward):
        copies = []
        for t in range(SUB):
            far = source.at[:, :, pl.ds(t * LANE, LANE)]
            near = target.at[:, pl.ds(t * strip, strip), :]
            copies.append(pltpu.make_async_copy(far, near, send.at[t]) if inward else pltpu.make_async_copy(near, far, send.at[t]))
        return copies

    def waves_copies(f):
        return natural(waves.at[0, f], nat.at[pl.ds(f * 4, 4)], in_sem.at[0, f], True)

    def surface_copies(f):
        return natural(surface.at[f], nat_surface.at[pl.ds(f * 4, 4)], in_sem.at[1, f], True)

    slow_copies = natural(slowness.at[0], nat_slow, in_sem.at[2, 0], True)
    for copy in slow_copies:
        copy.start()
    for f in range(fb):
        for copy in waves_copies(f):
            copy.start()

    @pl.when(s == 0)
    def _():
        for f in range(fb):
            for copy in surface_copies(f):
                copy.start()

    barrier = pltpu.get_barrier_semaphore()

    def greet(partner):
        pl.semaphore_signal(barrier, inc=1, device_id=partner, device_id_type=pl.DeviceIdType.MESH)

    for can_send, _, partner, _ in sides:
        run_if(can_send, functools.partial(greet, partner))
    run_if(has_next, functools.partial(greet, following))
    run_if(has_previous, functools.partial(greet, previous))

    def omega_tile(k):
        return jnp.full(TILE, 2.0 * math.pi * (BASE_HERTZ + HERTZ_STEP * k.astype(jnp.float32)), jnp.float32)

    for f in range(fb):
        omegas[f] = omega_tile(freqs[0, f])
    image[...] = jnp.zeros_like(image)
    if not folded:
        for f in range(fb):
            for buffer in (window, window2):
                buffer[f, :top] = jnp.zeros_like(buffer[f, :top])
                buffer[f, top + strip :] = jnp.zeros_like(buffer[f, top + strip :])
        slow[:top] = jnp.zeros_like(slow[:top])
        slow[top + strip :] = jnp.zeros_like(slow[top + strip :])
    for copy in slow_copies:
        copy.wait()
    for p in range(plane_count):
        for i in range(strip):
            slow[top + i, p] = nat_slow[p, pl.ds(place_of(i), SUB, stride=strip), :]

    peers = jnp.where(has_next, 1, 0) + jnp.where(has_previous, 1, 0)
    for can_send, _, _, _ in sides:
        peers = peers + (1 if can_send is None else jnp.where(can_send, 1, 0))
    pl.semaphore_wait(barrier, peers)

    omega_copy = pltpu.make_async_remote_copy(
        src_ref=omegas, dst_ref=omegas2, send_sem=omega_sem.at[0], recv_sem=omega_sem.at[1],
        device_id=following, device_id_type=pl.DeviceIdType.MESH,
    )
    halos(slow, slow_send, slow_recv, "start")
    run_if(has_next, omega_copy.start)

    def relayout(source, target, f):
        for i in range(strip):
            for c in range(4):
                target[f, top + i, c] = source[f * 4 + c, pl.ds(place_of(i), SUB, stride=strip), :]

    @pl.loop(0, fb)
    def _(f):
        for copy in waves_copies(f):
            copy.wait()
        relayout(nat, window, f)
        halos(window.at[f], halo_send.at[0, f], halo_recv.at[0, f], "start")

    row_of = lax.broadcasted_iota(jnp.int32, TILE, 0)
    lane_of = lax.broadcasted_iota(jnp.int32, TILE, 1)
    first_lane, last_lane = lane_of == 0, lane_of == LANE - 1
    first_row, last_row = row_of == 0, row_of == SUB - 1

    def beside(u):
        left = pltpu.roll(u, 1, 1)
        right = pltpu.roll(u, LANE - 1, 1)
        before = jnp.where(first_row, 0.0, pltpu.roll(left, 1, 0))
        after = jnp.where(last_row, 0.0, pltpu.roll(right, SUB - 1, 0))
        return jnp.where(first_lane, before, left) + jnp.where(last_lane, after, right)

    def section(load, omega):
        rate, g_re, g_im, k_re, k_im = constants_of(omega)

        def spread(u, total):
            s_re, s_im, r_re, r_im = u
            return (
                g_re * s_re - g_im * s_im + total[0],
                g_re * s_im + g_im * s_re + total[1],
                g_re * r_re + g_im * r_im + total[2],
                g_re * r_im - g_im * r_re + total[3],
            )

        def rotated(p, j):
            sin, cos = sin_cos((slow[j, p] - MIDDLE_SLOWNESS) * rate)
            e_re, e_im = k_re * cos - k_im * sin, k_re * sin + k_im * cos
            s_re, s_im, r_re, r_im = [load(j, c) if p == 0 else states[p - 1, j, c] for c in range(4)]
            return (
                s_re * e_re - s_im * e_im,
                s_re * e_im + s_im * e_re,
                r_re * e_re + r_im * e_im,
                r_im * e_re - r_re * e_im,
            )

        for p in range(plane_count):
            low, high = (0 if folded else p + 1), width - 1 - p
            behind = None if folded else rotated(p, low - 1)
            here = rotated(p, low)
            for j in range(low, high):
                ahead = rotated(p, j + 1)
                total = ahead if behind is None else [x + y for x, y in zip(behind, ahead)]
                u = spread(here, total)
                if j < top:
                    u = [jnp.where(l > 0, x, 0.0) for x in u]
                elif j >= top + strip and not folded:
                    u = [jnp.where(l < strips - 1, x, 0.0) for x in u]
                u = spread(u, [beside(x) for x in u])
                for c in range(4):
                    states[p, j, c] = u[c]
                if top <= j < top + strip:
                    image[p, j - top] += u[0] * u[2] + u[1] * u[3]
                behind, here = here, ahead

    last_plane = jnp.clip(planes_ref[0] - 1, 0, plane_count - 1)

    def depth_copy(f):
        return pltpu.make_async_remote_copy(
            src_ref=outgoing.at[f], dst_ref=window2.at[f, pl.ds(top, strip)],
            send_sem=depth_send.at[f], recv_sem=depth_recv.at[f],
            device_id=following, device_id_type=pl.DeviceIdType.MESH,
        )

    halos(slow, slow_send, slow_recv, "wait_recv")

    @pl.loop(0, fb)
    def _(f):
        halos(window.at[f], halo_send.at[0, f], halo_recv.at[0, f], "wait_recv")
        section(lambda j, c: window[f, j, c], omegas[f])
        for i in range(strip):
            for c in range(4):
                outgoing[f, i, c] = states[last_plane, top + i, c]

        @pl.when(has_next)
        def _():
            depth_copy(f).start()

    @pl.when(has_previous)
    def _():
        omega_copy.wait_recv()

    @pl.when(s == 0)
    def _():
        for f in range(fb):
            omegas2[f] = omega_tile(surface_freqs[f])

    def arrive(f):
        @pl.when(has_previous)
        def _():
            depth_copy(f).wait_recv()

        @pl.when(s == 0)
        def _():
            for copy in surface_copies(f):
                copy.wait()
            relayout(nat_surface, window2, f)

        halos(window2.at[f], halo_send.at[1, f], halo_recv.at[1, f], "start")

    def out_copies(f):
        return natural(waves_out.at[0, f], nat_out.at[pl.ds(f * 4, 4)], out_sem.at[f], False)

    arrive(0)

    @pl.loop(0, fb)
    def _(f):
        @pl.when(f < fb - 1)
        def _():
            arrive(f + 1)

        halos(window2.at[f], halo_send.at[1, f], halo_recv.at[1, f], "wait_recv")
        section(lambda j, c: window2[f, j, c], omegas2[f])
        for i in range(strip):
            for c in range(4):
                nat_out[f * 4 + c, pl.ds(place_of(i), SUB, stride=strip), :] = states[last_plane, top + i, c]
        for copy in out_copies(f):
            copy.start()

    for p in range(plane_count):
        weight = jnp.where(p <= last_plane, 1.0 / fb, 0.0)
        for i in range(strip):
            nat_image[p, pl.ds(place_of(i), SUB, stride=strip), :] = image[p, i] * weight
    image_copies = natural(image_out.at[0], nat_image, out_sem.at[fb], False)
    for copy in image_copies:
        copy.start()
    halos(slow, slow_send, slow_recv, "wait_send")

    @pl.when(has_next)
    def _():
        omega_copy.wait_send()
        for f in range(fb):
            depth_copy(f).wait_send()

    for f in range(fb):
        halos(window.at[f], halo_send.at[0, f], halo_recv.at[0, f], "wait_send")
        halos(window2.at[f], halo_send.at[1, f], halo_recv.at[1, f], "wait_send")
        for copy in out_copies(f):
            copy.wait()
    for copy in image_copies:
        copy.wait()


def local(waves_in, surface_waves, slowness, section_planes, block_freqs, surface_freqs):
    axes = (lax.axis_size("depth"), lax.axis_size("lat"))
    _, fb, _, strip, columns = waves_in.shape
    plane_count = slowness.shape[1]
    if columns != SUB * LANE or strip != SUB:
        raise ValueError("unsupported strip")
    folded = axes[1] == 2
    width = (0 if folded else plane_count) + strip + plane_count
    per_halo = plane_count if folded else 2
    f32 = jnp.float32
    dma = pltpu.SemaphoreType.DMA
    anywhere = pl.BlockSpec(memory_space=pl.ANY)
    scalars = pl.BlockSpec(memory_space=pltpu.SMEM)
    return pl.pallas_call(
        functools.partial(kernel, axes),
        out_shape=(jax.ShapeDtypeStruct(waves_in.shape, f32), jax.ShapeDtypeStruct(slowness.shape, f32)),
        in_specs=[anywhere] * 3 + [scalars] * 3,
        out_specs=(anywhere, anywhere),
        scratch_shapes=[
            pltpu.VMEM((fb * 4, SUB * strip, LANE), f32),
            pltpu.VMEM((fb * 4, SUB * strip, LANE), f32),
            pltpu.VMEM((plane_count, SUB * strip, LANE), f32),
            pltpu.VMEM((fb, width, 4) + TILE, f32),
            pltpu.VMEM((fb, width, 4) + TILE, f32),
            pltpu.VMEM((width, plane_count) + TILE, f32),
            pltpu.VMEM((plane_count, width, 4) + TILE, f32),
            pltpu.VMEM((fb, strip, 4) + TILE, f32),
            pltpu.VMEM((fb,) + TILE, f32),
            pltpu.VMEM((fb,) + TILE, f32),
            pltpu.VMEM((plane_count, strip) + TILE, f32),
            pltpu.VMEM((fb * 4, SUB * strip, LANE), f32),
            pltpu.VMEM((plane_count, SUB * strip, LANE), f32),
            dma((3, fb, SUB)),
            dma((fb + 1, SUB)),
            dma((per_halo,)),
            dma((per_halo,)),
            dma((2, fb, per_halo)),
            dma((2, fb, per_halo)),
            dma((fb,)),
            dma((fb,)),
            dma((2,)),
        ],
        compiler_params=pltpu.CompilerParams(collective_id=0, has_side_effects=True),
        name="migrate",
    )(waves_in, surface_waves, slowness, section_planes, block_freqs, surface_freqs)


def solution(mesh):
    return jax.shard_map(
        local,
        mesh=mesh,
        in_specs=(
            P("depth", None, None, "lat", None),
            P(None, None, "lat", None),
            P("depth", None, "lat", None),
            P("depth"),
            P("depth", None),
            P(),
        ),
        out_specs=(P("depth", None, None, "lat", None), P("depth", None, "lat", None)),
        check_vma=False,
    )
```

time: 79.3 us -> 30.3 us (0.38)
  the two profiles are of different devices: /device:TPU:8 before, /device:TPU:0 now
where the time goes in v1:
time: 30.3 us; the launch traced here: 30.1 us
  Pallas kernels  26.2 us (86%)
  local copies, waits for them, and re-layouts  2.58 us (9%)
  between operations  1.29 us (4%)
    pallas_call x1, Pallas kernels, local(): pl.pallas_call(functools.partial(kernel, axes), out_shape=(jax.ShapeDtype...  26.2 us
    unnamed x4, local copies, waits for them, and re-layouts  2.58 us

profile of v1, /device:TPU:0, one launch (start us, length us, event | category | flops | bytes accessed | tf_op | source)
XLA Modules:
  0.0 30.1 jit_solution(15808946076511424658)
XLA Ops:
  1.3 26.2 %migrate.1 = (f32[1,4,4,8,1024]{4,3,2,1,0:T(8,128)}, f32[1,4,8,1024]{3,2,1,0:T(8,128)}) custom-call(f32[1,4,4,8,1024]{4,3,2,1,0:T(8,128)} %waves.1, f32[4,4,8,1024]{3,2,1,0:T(8,128)} %surface.1, f32[1,4,8,1024]{3,2,1,0:T(8,128)} %slowness.1, s32[1]{0:T(128)S(6)} %copy.10.planes_ref, s32[1,4]{1,0:T(1,128)} %freqs.1, s32[4]{0:T(128)} %surface_freqs.1), custom_call_target="tpu_custom_call" | custom-call | tf_op jit(solution)/shard_map/migrate/pallas_call | solution.py:340
  27.5 0.0 copy-start
  27.5 1.9 %copy.11 = f32[1,4,4,8,1024]{4,3,2,1,0:T(8,128)} copy(f32[1,4,4,8,1024]{4,3,2,1,0:T(8,128)} %get-tuple-element.4) | data formatting | bytes 1048576
  29.4 0.0 copy-done
  29.4 0.7 %copy.12 = f32[1,4,8,1024]{3,2,1,0:T(8,128)} copy(f32[1,4,8,1024]{3,2,1,0:T(8,128)S(1)} %copy-done) | data formatting | bytes 262144
Async XLA Ops:
  27.5 1.9 %copy-start = (f32[1,4,8,1024]{3,2,1,0:T(8,128)S(1)}, f32[1,4,8,1024]{3,2,1,0:T(8,128)}, u32[]{:S(2)}) copy-start(f32[1,4,8,1024]{3,2,1,0:T(8,128)} %get-tuple-element.5) | copy-start | bytes 393220

commit v2 on v1

--- a/solution.py
+++ b/solution.py
@@ -77,20 +77,23 @@
         else:
             pl.when(condition)(body)
 
-    def halo_copies(source, target, send, recv, partner, copies, first):
+    def halo_copies(buffer, send, recv, partner, copies, first, trimmed):
+        def view(row, rows, i):
+            return buffer.at[pl.ds(row, rows), pl.ds(0, plane_count - i)] if trimmed and folded else buffer.at[pl.ds(row, rows)]
+
         return [
             pltpu.make_async_remote_copy(
-                src_ref=source.at[pl.ds(row, rows)], dst_ref=target.at[pl.ds(place, rows)],
+                src_ref=view(row, rows, i), dst_ref=view(place, rows, i),
                 send_sem=send.at[first + i], recv_sem=recv.at[first + i],
                 device_id=partner, device_id_type=pl.DeviceIdType.MESH,
             )
             for i, (row, place, rows) in enumerate(copies)
         ]
 
-    def halos(buffer, send, recv, action):
+    def halos(buffer, send, recv, action, trimmed=False):
         first = 0
         for can_send, can_receive, partner, copies in sides:
-            descriptors = halo_copies(buffer, buffer, send, recv, partner, copies, first)
+            descriptors = halo_copies(buffer, send, recv, partner, copies, first, trimmed)
             first += len(copies)
 
             def act(descriptors=descriptors):
@@ -167,7 +170,7 @@
         src_ref=omegas, dst_ref=omegas2, send_sem=omega_sem.at[0], recv_sem=omega_sem.at[1],
         device_id=following, device_id_type=pl.DeviceIdType.MESH,
     )
-    halos(slow, slow_send, slow_recv, "start")
+    halos(slow, slow_send, slow_recv, "start", True)
     run_if(has_next, omega_copy.start)
 
     def relayout(source, target, f):
@@ -245,7 +248,7 @@
             device_id=following, device_id_type=pl.DeviceIdType.MESH,
         )
 
-    halos(slow, slow_send, slow_recv, "wait_recv")
+    halos(slow, slow_send, slow_recv, "wait_recv", True)
 
     @pl.loop(0, fb)
     def _(f):
@@ -307,7 +310,7 @@
     image_copies = natural(image_out.at[0], nat_image, out_sem.at[fb], False)
     for copy in image_copies:
         copy.start()
-    halos(slow, slow_send, slow_recv, "wait_send")
+    halos(slow, slow_send, slow_recv, "wait_send", True)
 
     @pl.when(has_next)
     def _():
@@ -340,7 +343,7 @@
     return pl.pallas_call(
         functools.partial(kernel, axes),
         out_shape=(jax.ShapeDtypeStruct(waves_in.shape, f32), jax.ShapeDtypeStruct(slowness.shape, f32)),
-        in_specs=[anywhere] * 3 + [scalars] * 3,
+        in_specs=[pl.BlockSpec(memory_space=pltpu.HBM)] * 3 + [scalars] * 3,
         out_specs=(anywhere, anywhere),
         scratch_shapes=[
             pltpu.VMEM((fb * 4, SUB * strip, LANE), f32),
@@ -366,7 +369,7 @@
             dma((fb,)),
             dma((2,)),
         ],
-        compiler_params=pltpu.CompilerParams(collective_id=0, has_side_effects=True),
+        compiler_params=pltpu.CompilerParams(collective_id=0, has_side_effects=True, vmem_limit_bytes=32 << 20),
         name="migrate",
     )(waves_in, surface_waves, slowness, section_planes, block_freqs, surface_freqs)
 

time: 30.3 us -> 30.3 us (level)
  Pallas kernels: 26.2 us -> 24.2 us
  local copies, waits for them, and re-layouts: 2.58 us -> 4.44 us
    pallas_call x1, Pallas kernels: 26.2 us -> 24.2 us  [local(): pl.pallas_call(functools.partial(kernel, axes), out_shape=(jax.ShapeDtype...]
    unnamed x4 -> x12, local copies, waits for them, and re-layouts: 2.58 us -> 4.44 us
where the time goes in v2:
time: 30.3 us; the launch traced here: 30 us
  Pallas kernels  24.2 us (80%)
  local copies, waits for them, and re-layouts  4.44 us (15%)
  between operations  1.35 us (4%)
    pallas_call x1, Pallas kernels, local(): pl.pallas_call(functools.partial(kernel, axes), out_shape=(jax.ShapeDtype...  24.2 us
    unnamed x12, local copies, waits for them, and re-layouts  4.44 us

profile of v2, /device:TPU:0, one launch (start us, length us, event | category | flops | bytes accessed | tf_op | source)
XLA Modules:
  0.0 30.0 jit_solution(12877000293029128810)
XLA Ops:
  0.6 0.0 copy-start.4
  0.6 0.0 copy-start.3
  1.3 0.0 copy-done.4
  1.3 0.0 copy-done.3
  1.3 0.0 copy-start
  1.3 1.0 %copy-done = f32[1,4,4,8,1024]{4,3,2,1,0:T(8,128)S(1)} copy-done((f32[1,4,4,8,1024]{4,3,2,1,0:T(8,128)S(1)}, f32[1,4,4,8,1024]{4,3,2,1,0:T(8,128)}, u32[]{:S(2)}) %copy-start) | copy-done | bytes 524312
  2.4 0.0 copy-start.1
  2.4 1.0 %copy-done.1 = f32[4,4,8,1024]{3,2,1,0:T(8,128)S(1)} copy-done((f32[4,4,8,1024]{3,2,1,0:T(8,128)S(1)}, f32[4,4,8,1024]{3,2,1,0:T(8,128)}, u32[]{:S(2)}) %copy-start.1) | copy-done | bytes 524312
  3.4 0.0 copy-start.2
  3.4 0.9 %copy-done.2 = f32[1,4,8,1024]{3,2,1,0:T(8,128)S(1)} copy-done((f32[1,4,8,1024]{3,2,1,0:T(8,128)S(1)}, f32[1,4,8,1024]{3,2,1,0:T(8,128)}, u32[]{:S(2)}) %copy-start.2) | copy-done | bytes 131096
  4.3 24.2 %migrate.1 = (f32[1,4,4,8,1024]{4,3,2,1,0:T(8,128)S(1)}, f32[1,4,8,1024]{3,2,1,0:T(8,128)S(1)}) custom-call(f32[1,4,4,8,1024]{4,3,2,1,0:T(8,128)S(1)} %copy-done, f32[4,4,8,1024]{3,2,1,0:T(8,128)S(1)} %copy-done.1, f32[1,4,8,1024]{3,2,1,0:T(8,128)S(1)} %copy-done.2, s32[1]{0:T(128)S(6)} %copy.10.planes_ref, s32[1,4]{1,0:T(1,128)S(1)} %copy-done.3, ...), custom_call_target="tpu_custom_call" | custom-call | tf_op jit(solution)/shard_map/migrate/pallas_call | solution.py:343
  28.6 0.8 %copy.11 = f32[1,4,4,8,1024]{4,3,2,1,0:T(8,128)} copy(f32[1,4,4,8,1024]{4,3,2,1,0:T(8,128)S(1)} %get-tuple-element.4) | data formatting | bytes 1048576
  29.4 0.7 %copy.12 = f32[1,4,8,1024]{3,2,1,0:T(8,128)} copy(f32[1,4,8,1024]{3,2,1,0:T(8,128)S(1)} %get-tuple-element.5) | data formatting | bytes 262144
Async XLA Ops:
  0.6 0.7 %copy-start.4 = (s32[4]{0:T(128)S(1)}, s32[4]{0:T(128)}, u32[]{:S(2)}) copy-start(s32[4]{0:T(128)} %surface_freqs.1) | copy-start | bytes 52
  0.6 0.7 %copy-start.3 = (s32[1,4]{1,0:T(1,128)S(1)}, s32[1,4]{1,0:T(1,128)}, u32[]{:S(2)}) copy-start(s32[1,4]{1,0:T(1,128)} %freqs.1) | copy-start | bytes 52
  1.3 1.0 %copy-start = (f32[1,4,4,8,1024]{4,3,2,1,0:T(8,128)S(1)}, f32[1,4,4,8,1024]{4,3,2,1,0:T(8,128)}, u32[]{:S(2)}) copy-start(f32[1,4,4,8,1024]{4,3,2,1,0:T(8,128)} %waves.1) | copy-start | bytes 1572868
  2.4 1.0 %copy-start.1 = (f32[4,4,8,1024]{3,2,1,0:T(8,128)S(1)}, f32[4,4,8,1024]{3,2,1,0:T(8,128)}, u32[]{:S(2)}) copy-start(f32[4,4,8,1024]{3,2,1,0:T(8,128)} %surface.1) | copy-start | bytes 1572868
  3.4 0.9 %copy-start.2 = (f32[1,4,8,1024]{3,2,1,0:T(8,128)S(1)}, f32[1,4,8,1024]{3,2,1,0:T(8,128)}, u32[]{:S(2)}) copy-start(f32[1,4,8,1024]{3,2,1,0:T(8,128)} %slowness.1) | copy-start | bytes 393220

commit v3 on v2

--- a/solution.py
+++ b/solution.py
@@ -46,9 +46,9 @@
 
 
 def kernel(
-    axes, waves, surface, slowness, planes_ref, freqs, surface_freqs, waves_out, image_out,
-    nat, nat_surface, nat_slow, window, window2, slow, states, outgoing, omegas, omegas2, image, nat_out, nat_image,
-    in_sem, out_sem, slow_send, slow_recv, halo_send, halo_recv, depth_send, depth_recv, omega_sem,
+    axes, waves, surface, slowness, planes_ref, freqs, surface_freqs, nat_out, nat_image,
+    nat, nat_surface, nat_slow, window, window2, slow, states, outgoing, omegas, omegas2, image,
+    in_sem, slow_send, slow_recv, halo_send, halo_recv, depth_send, depth_recv, omega_sem,
 ):
     sections, strips = axes
     s, l = lax.axis_index("depth"), lax.axis_index("lat")
@@ -105,21 +105,19 @@
     def place_of(i):
         return i + l * (strip - 1 - 2 * i) if folded else i
 
-    def natural(source, target, send, inward):
-        copies = []
-        for t in range(SUB):
-            far = source.at[:, :, pl.ds(t * LANE, LANE)]
-            near = target.at[:, pl.ds(t * strip, strip), :]
-            copies.append(pltpu.make_async_copy(far, near, send.at[t]) if inward else pltpu.make_async_copy(near, far, send.at[t]))
-        return copies
+    def natural(source, target, send):
+        return [
+            pltpu.make_async_copy(source.at[:, :, pl.ds(t * LANE, LANE)], target.at[:, pl.ds(t * strip, strip), :], send.at[t])
+            for t in range(SUB)
+        ]
 
     def waves_copies(f):
-        return natural(waves.at[0, f], nat.at[pl.ds(f * 4, 4)], in_sem.at[0, f], True)
+        return natural(waves.at[0, f], nat.at[pl.ds(f * 4, 4)], in_sem.at[0, f])
 
     def surface_copies(f):
-        return natural(surface.at[f], nat_surface.at[pl.ds(f * 4, 4)], in_sem.at[1, f], True)
-
-    slow_copies = natural(slowness.at[0], nat_slow, in_sem.at[2, 0], True)
+        return natural(surface.at[f], nat_surface.at[pl.ds(f * 4, 4)], in_sem.at[1, f])
+
+    slow_copies = natural(slowness.at[0], nat_slow, in_sem.at[2, 0])
     for copy in slow_copies:
         copy.start()
     for f in range(fb):
@@ -284,9 +282,6 @@
 
         halos(window2.at[f], halo_send.at[1, f], halo_recv.at[1, f], "start")
 
-    def out_copies(f):
-        return natural(waves_out.at[0, f], nat_out.at[pl.ds(f * 4, 4)], out_sem.at[f], False)
-
     arrive(0)
 
     @pl.loop(0, fb)
@@ -300,16 +295,11 @@
         for i in range(strip):
             for c in range(4):
                 nat_out[f * 4 + c, pl.ds(place_of(i), SUB, stride=strip), :] = states[last_plane, top + i, c]
-        for copy in out_copies(f):
-            copy.start()
 
     for p in range(plane_count):
         weight = jnp.where(p <= last_plane, 1.0 / fb, 0.0)
         for i in range(strip):
             nat_image[p, pl.ds(place_of(i), SUB, stride=strip), :] = image[p, i] * weight
-    image_copies = natural(image_out.at[0], nat_image, out_sem.at[fb], False)
-    for copy in image_copies:
-        copy.start()
     halos(slow, slow_send, slow_recv, "wait_send", True)
 
     @pl.when(has_next)
@@ -321,10 +311,6 @@
     for f in range(fb):
         halos(window.at[f], halo_send.at[0, f], halo_recv.at[0, f], "wait_send")
         halos(window2.at[f], halo_send.at[1, f], halo_recv.at[1, f], "wait_send")
-        for copy in out_copies(f):
-            copy.wait()
-    for copy in image_copies:
-        copy.wait()
 
 
 def local(waves_in, surface_waves, slowness, section_planes, block_freqs, surface_freqs):
@@ -340,11 +326,11 @@
     dma = pltpu.SemaphoreType.DMA
     anywhere = pl.BlockSpec(memory_space=pl.ANY)
     scalars = pl.BlockSpec(memory_space=pltpu.SMEM)
-    return pl.pallas_call(
+    waves_out, image = pl.pallas_call(
         functools.partial(kernel, axes),
-        out_shape=(jax.ShapeDtypeStruct(waves_in.shape, f32), jax.ShapeDtypeStruct(slowness.shape, f32)),
+        out_shape=(pltpu.VMEM((fb * 4, SUB * strip, LANE), f32), pltpu.VMEM((plane_count, SUB * strip, LANE), f32)),
         in_specs=[pl.BlockSpec(memory_space=pltpu.HBM)] * 3 + [scalars] * 3,
-        out_specs=(anywhere, anywhere),
+        out_specs=(pl.BlockSpec(memory_space=pltpu.VMEM),) * 2,
         scratch_shapes=[
             pltpu.VMEM((fb * 4, SUB * strip, LANE), f32),
             pltpu.VMEM((fb * 4, SUB * strip, LANE), f32),
@@ -357,10 +343,7 @@
             pltpu.VMEM((fb,) + TILE, f32),
             pltpu.VMEM((fb,) + TILE, f32),
             pltpu.VMEM((plane_count, strip) + TILE, f32),
-            pltpu.VMEM((fb * 4, SUB * strip, LANE), f32),
-            pltpu.VMEM((plane_count, SUB * strip, LANE), f32),
             dma((3, fb, SUB)),
-            dma((fb + 1, SUB)),
             dma((per_halo,)),
             dma((per_halo,)),
             dma((2, fb, per_halo)),
@@ -371,7 +354,12 @@
         ],
         compiler_params=pltpu.CompilerParams(collective_id=0, has_side_effects=True, vmem_limit_bytes=32 << 20),
         name="migrate",
-    )(waves_in, surface_waves, slowness, section_planes, block_freqs, surface_freqs)
+    )(*[pltpu.with_memory_space_constraint(x, pltpu.HBM) for x in (waves_in, surface_waves, slowness)], section_planes, block_freqs, surface_freqs)
+
+    def rows_first(x, shape):
+        return x.reshape(-1, SUB, strip, LANE).swapaxes(1, 2).reshape(shape)
+
+    return rows_first(waves_out, waves_in.shape), rows_first(image, slowness.shape)
 
 
 def solution(mesh):

time: 30.3 us -> 27.5 us (0.908)
  local copies, waits for them, and re-layouts: 4.44 us -> 1.46 us
    unnamed x12 -> x6, local copies, waits for them, and re-layouts: 4.44 us -> 1.46 us
    pallas_call x1, Pallas kernels: 24.2 us -> 24.5 us  [local(): pl.pallas_call(functools.partial(kernel, axes), out_shape=(pltpu.VMEM((fb...]
where the time goes in v3:
time: 27.5 us; the launch traced here: 27.3 us
  Pallas kernels  24.5 us (89%)
  local copies, waits for them, and re-layouts  1.46 us (5%)
  between operations  1.34 us (5%)
    pallas_call x1, Pallas kernels, local(): pl.pallas_call(functools.partial(kernel, axes), out_shape=(pltpu.VMEM((fb...  24.5 us
    unnamed x6, local copies, waits for them, and re-layouts  1.46 us

profile of v3, /device:TPU:0, one launch (start us, length us, event | category | flops | bytes accessed | tf_op | source)
XLA Modules:
  0.0 27.3 jit_solution(1063426924751575495)
XLA Ops:
  0.6 0.0 copy-start.1
  0.6 0.0 copy-start
  1.3 0.0 copy-done.1
  1.3 0.0 copy-done
  1.3 24.5 %migrate.1 = (f32[16,64,128]{2,1,0:T(8,128)S(1)}, f32[4,64,128]{2,1,0:T(8,128)S(1)}) custom-call(f32[1,4,4,8,1024]{4,3,2,1,0:T(8,128)} %waves.1, f32[4,4,8,1024]{3,2,1,0:T(8,128)} %surface.1, f32[1,4,8,1024]{3,2,1,0:T(8,128)} %slowness.1, s32[1]{0:T(128)S(6)} %copy.12.planes_ref, s32[1,4]{1,0:T(1,128)S(1)} %copy-done, s32[4]{0:T(128)S(1)} %copy-done.1), custom_call_target="tpu_custom_call" | custom-call | tf_op jit(solution)/shard_map/migrate/pallas_call | solution.py:329
  25.9 0.8 %copy.10 = f32[1,4,4,8,1024]{4,3,2,1,0:T(8,128)} copy(f32[1,4,4,8,1024]{4,3,2,1,0:T(8,128)S(1)} %bitcast.10) | data formatting | bytes 1048576
  26.7 0.7 %copy.11 = f32[1,4,8,1024]{3,2,1,0:T(8,128)} copy(f32[1,4,8,1024]{3,2,1,0:T(8,128)S(1)} %bitcast.11) | data formatting | bytes 262144
Async XLA Ops:
  0.6 0.7 %copy-start.1 = (s32[4]{0:T(128)S(1)}, s32[4]{0:T(128)}, u32[]{:S(2)}) copy-start(s32[4]{0:T(128)} %surface_freqs.1) | copy-start | bytes 52
  0.6 0.7 %copy-start = (s32[1,4]{1,0:T(1,128)S(1)}, s32[1,4]{1,0:T(1,128)}, u32[]{:S(2)}) copy-start(s32[1,4]{1,0:T(1,128)} %freqs.1) | copy-start | bytes 52

commit v4 on v3

--- a/solution.py
+++ b/solution.py
@@ -239,12 +239,32 @@
 
     last_plane = jnp.clip(planes_ref[0] - 1, 0, plane_count - 1)
 
-    def depth_copy(f):
-        return pltpu.make_async_remote_copy(
-            src_ref=outgoing.at[f], dst_ref=window2.at[f, pl.ds(top, strip)],
-            send_sem=depth_send.at[f], recv_sem=depth_recv.at[f],
-            device_id=following, device_id_type=pl.DeviceIdType.MESH,
-        )
+    pieces = [(strip - halo, halo), (0, strip - halo)] if folded and halo < strip else [(0, strip)]
+
+    def depth_copies(f):
+        return [
+            pltpu.make_async_remote_copy(
+                src_ref=outgoing.at[f, pl.ds(row, rows)], dst_ref=window2.at[f, pl.ds(top + row, rows)],
+                send_sem=depth_send.at[f, k], recv_sem=depth_recv.at[f, k],
+                device_id=following, device_id_type=pl.DeviceIdType.MESH,
+            )
+            for k, (row, rows) in enumerate(pieces)
+        ]
+
+    def arrive(f):
+        @pl.when(has_previous)
+        def _():
+            depth_copies(f)[0].wait_recv()
+
+        @pl.when(s == 0)
+        def _():
+            for copy in surface_copies(f):
+                copy.wait()
+            relayout(nat_surface, window2, f)
+
+        halos(window2.at[f], halo_send.at[1, f], halo_recv.at[1, f], "start")
+
+    lag = min(2, fb)
 
     halos(slow, slow_send, slow_recv, "wait_recv", True)
 
@@ -258,7 +278,12 @@
 
         @pl.when(has_next)
         def _():
-            depth_copy(f).start()
+            for copy in depth_copies(f):
+                copy.start()
+
+        @pl.when(f >= lag)
+        def _():
+            arrive(f - lag)
 
     @pl.when(has_previous)
     def _():
@@ -269,26 +294,19 @@
         for f in range(fb):
             omegas2[f] = omega_tile(surface_freqs[f])
 
-    def arrive(f):
-        @pl.when(has_previous)
-        def _():
-            depth_copy(f).wait_recv()
-
-        @pl.when(s == 0)
-        def _():
-            for copy in surface_copies(f):
-                copy.wait()
-            relayout(nat_surface, window2, f)
-
-        halos(window2.at[f], halo_send.at[1, f], halo_recv.at[1, f], "start")
-
-    arrive(0)
+    for f in range(fb - lag, lag):
+        arrive(f)
 
     @pl.loop(0, fb)
     def _(f):
-        @pl.when(f < fb - 1)
-        def _():
-            arrive(f + 1)
+        @pl.when(f < fb - lag)
+        def _():
+            arrive(f + lag)
+
+        @pl.when(has_previous)
+        def _():
+            for copy in depth_copies(f)[1:]:
+                copy.wait_recv()
 
         halos(window2.at[f], halo_send.at[1, f], halo_recv.at[1, f], "wait_recv")
         section(lambda j, c: window2[f, j, c], omegas2[f])
@@ -306,7 +324,8 @@
     def _():
         omega_copy.wait_send()
         for f in range(fb):
-            depth_copy(f).wait_send()
+            for copy in depth_copies(f):
+                copy.wait_send()
 
     for f in range(fb):
         halos(window.at[f], halo_send.at[0, f], halo_recv.at[0, f], "wait_send")
@@ -348,8 +367,8 @@
             dma((per_halo,)),
             dma((2, fb, per_halo)),
             dma((2, fb, per_halo)),
-            dma((fb,)),
-            dma((fb,)),
+            dma((fb, 2)),
+            dma((fb, 2)),
             dma((2,)),
         ],
         compiler_params=pltpu.CompilerParams(collective_id=0, has_side_effects=True, vmem_limit_bytes=32 << 20),

time: 27.5 us -> 24.7 us (0.90)
  Pallas kernels: 24.5 us -> 21.8 us
    pallas_call x1, Pallas kernels: 24.5 us -> 21.8 us  [local(): pl.pallas_call(functools.partial(kernel, axes), out_shape=(pltpu.VMEM((fb...]
where the time goes in v4:
time: 24.7 us; the launch traced here: 24.6 us
  Pallas kernels  21.8 us (88%)
  local copies, waits for them, and re-layouts  1.46 us (6%)
  between operations  1.34 us (5%)
    pallas_call x1, Pallas kernels, local(): pl.pallas_call(functools.partial(kernel, axes), out_shape=(pltpu.VMEM((fb...  21.8 us
    unnamed x6, local copies, waits for them, and re-layouts  1.46 us

profile of v4, /device:TPU:0, one launch (start us, length us, event | category | flops | bytes accessed | tf_op | source)
XLA Modules:
  0.0 24.6 jit_solution(4745002294156326245)
XLA Ops:
  0.6 0.0 copy-start.1
  0.6 0.0 copy-start
  1.3 0.0 copy-done.1
  1.3 0.0 copy-done
  1.3 21.8 %migrate.1 = (f32[16,64,128]{2,1,0:T(8,128)S(1)}, f32[4,64,128]{2,1,0:T(8,128)S(1)}) custom-call(f32[1,4,4,8,1024]{4,3,2,1,0:T(8,128)} %waves.1, f32[4,4,8,1024]{3,2,1,0:T(8,128)} %surface.1, f32[1,4,8,1024]{3,2,1,0:T(8,128)} %slowness.1, s32[1]{0:T(128)S(6)} %copy.12.planes_ref, s32[1,4]{1,0:T(1,128)S(1)} %copy-done, s32[4]{0:T(128)S(1)} %copy-done.1), custom_call_target="tpu_custom_call" | custom-call | tf_op jit(solution)/shard_map/migrate/pallas_call | solution.py:348
  23.1 0.8 %copy.10 = f32[1,4,4,8,1024]{4,3,2,1,0:T(8,128)} copy(f32[1,4,4,8,1024]{4,3,2,1,0:T(8,128)S(1)} %bitcast.10) | data formatting | bytes 1048576
  23.9 0.7 %copy.11 = f32[1,4,8,1024]{3,2,1,0:T(8,128)} copy(f32[1,4,8,1024]{3,2,1,0:T(8,128)S(1)} %bitcast.11) | data formatting | bytes 262144
Async XLA Ops:
  0.6 0.7 %copy-start.1 = (s32[4]{0:T(128)S(1)}, s32[4]{0:T(128)}, u32[]{:S(2)}) copy-start(s32[4]{0:T(128)} %surface_freqs.1) | copy-start | bytes 52
  0.6 0.7 %copy-start = (s32[1,4]{1,0:T(1,128)S(1)}, s32[1,4]{1,0:T(1,128)}, u32[]{:S(2)}) copy-start(s32[1,4]{1,0:T(1,128)} %freqs.1) | copy-start | bytes 52
